TPU v7x, 128 devices: a whole 4x4x4 slice. The times are simulated.
128 devices in a mesh: head: 4 (over z_lo, core), track: 32 (over y, z_hi, x).
Axes of the slice: x: 4, y: 4, z: 4 (z_hi: 2, z_lo: 2; z = z_hi * 2 + z_lo), core: 2. Of those that a mesh axis runs over, the one named last changes fastest.
Arguments:
- potential: float32 [256, 4096, 128], P('head', 'track'), may hold values from -6 to 6
- source: float32 [256, 4096, 128], P('head', 'track'), may hold values from -6 to 6
- depth_kernel: float32 [3, 128], replicated, may hold values from -0.5 to 0.5
- magnet: float32 [3, 32, 16384], P(None, 'track', 'head'), may hold values from -0.8 to 0.8
- footprint: int32 [32, 16384], P('track', 'head'), may hold values from 0 to 262143, as said below
- temp_index: int32 [32, 16384], P('track', 'head'), may hold values from 0 to 127
- temp_profile: float32 [128], replicated, may hold values from 0.3 to 1.4
- self_tiles: float32 [32, 128, 128, 128], P('track', 'head'), may hold values from -0.5 to 0.5
- next_tiles: float32 [32, 128, 128, 128], P('track', 'head'), may hold values from -0.5 to 0.5
Outputs:
- relaxed: float32 [256, 4096, 128], P('head', 'track')
- magnet_out: float32 [3, 32, 16384], P(None, 'track', 'head')
Inputs may be any that keep to these rules, and one draw needn't show every extreme that they name: Within the 4096 grains of one device (an aligned block of a track tile), no more than 256 have footprint cells in any one pole block of 8192 cells; in every draw one pole block, the same for every device, takes exactly 256 grains of every device.
All inputs are finite; a program needn't handle non-finite values.
Results may differ from a plain program's by a relative error of at most 0.0001.
Values sent between devices are 32-bit elements; how exact they have to be, the bound alone decides.
A program may use at most 320 MiB of HBM per device.

v0:
```python
import jax
import jax.numpy as jnp
from jax import lax
from jax.sharding import PartitionSpec as P

HIGH = lax.Precision.HIGHEST


def extended(block, sides, width):
    for axis, dim in sides:
        count = lax.axis_size(axis)
        forward = [(i, i + 1) for i in range(count - 1)]
        backward = [(target, source) for source, target in forward]
        low = lax.ppermute(
            lax.slice_in_dim(block, block.shape[dim] - width, None, axis=dim), axis, forward
        )
        high = lax.ppermute(lax.slice_in_dim(block, 0, width, axis=dim), axis, backward)
        block = jnp.concatenate([low, block, high], axis=dim)
    return block


def relax_sweep(padded, source):
    center = padded[1:-1, 1:-1]
    deep = jnp.pad(center, ((0, 0), (0, 0), (1, 1)))
    others = [
        padded[2:, 1:-1],
        padded[:-2, 1:-1],
        padded[1:-1, 2:],
        padded[1:-1, :-2],
        deep[:, :, 2:],
        deep[:, :, :-2],
    ]
    numer = source
    denom = jnp.ones_like(center)
    for other in others:
        differ = other - center
        perm = 1.0 + 4.0 / (1.0 + 4.0 * differ * differ)
        numer = numer + perm * differ
        denom = denom + perm
    return center + 0.8 * numer / denom


def cross_comp(a_vec, b_vec):
    return jnp.stack(
        [
            a_vec[1] * b_vec[2] - a_vec[2] * b_vec[1],
            a_vec[2] * b_vec[0] - a_vec[0] * b_vec[2],
            a_vec[0] * b_vec[1] - a_vec[1] * b_vec[0],
        ]
    )


def llb_section(state, field, target):
    sq_norm = jnp.sum(state * state, axis=0)
    total = field + 0.5 * (1.0 - sq_norm / target) * state
    turn = cross_comp(state, total)
    damp = cross_comp(state, turn)
    along = jnp.sum(state * total, axis=0)
    return state + 0.1 * (-turn - 0.5 * damp + 0.3 * along * state)


def per_device(
    potential,
    source,
    depth_kernel,
    magnet,
    footprint,
    temp_index,
    temp_profile,
    self_tiles,
    next_tiles,
):
    rows_x, rows_y, depth = potential.shape
    relaxed = potential
    for sweep_idx in range(2):
        padded = extended(relaxed, (("head", 0), ("track", 1)), 1)
        relaxed = relax_sweep(padded, source)
    surface = jnp.einsum("kz,xyz->kxy", depth_kernel, relaxed, precision=HIGH).reshape(
        3, rows_x * rows_y
    )
    cells = footprint[0]
    table = lax.all_gather(surface, "track", axis=1, tiled=True)
    applied = jnp.take(table, cells, axis=1)
    n_prof = temp_profile.shape[0]
    onehot = (temp_index[0][None, :] == jnp.arange(n_prof, dtype=jnp.int32)[:, None]).astype(
        jnp.float32
    )
    temp = jnp.dot(temp_profile[None, :], onehot, precision=HIGH)[0]
    target = 0.05 + jnp.maximum(1.0 - temp, 0.0)
    couple_self = self_tiles[0]
    couple_next = next_tiles[0]
    n_tiles, tile_w = (couple_self.shape[0], couple_self.shape[1])
    state = magnet[:, 0, :]
    for section in range(2):
        rimmed = extended(state, (("head", 1),), tile_w)
        tiles = rimmed.reshape(3, n_tiles + 2, tile_w)
        ex = jnp.einsum("kij,ckj->cki", couple_self, tiles[:, 1:-1], precision=HIGH)
        ex = ex + jnp.einsum("kij,ckj->cki", couple_next, tiles[:, :-2], precision=HIGH)
        ex = ex + jnp.einsum("kji,ckj->cki", couple_next, tiles[:, 2:], precision=HIGH)
        state = llb_section(state, applied + ex.reshape(3, n_tiles * tile_w), target)
    return (relaxed, state[:, None, :])


def solution(mesh):
    in_specs = (
        P("head", "track", None),
        P("head", "track", None),
        P(),
        P(None, "track", "head"),
        P("track", "head"),
        P("track", "head"),
        P(),
        P("track", "head", None, None),
        P("track", "head", None, None),
    )
    out_specs = (P("head", "track", None), P(None, "track", "head"))
    return jax.shard_map(
        per_device, mesh=mesh, in_specs=in_specs, out_specs=out_specs, check_vma=False
    )
```

profile of v0, /device:TPU:1, one launch (start us, length us, event | category | flops | bytes accessed | tf_op | source)
XLA Modules:
  0.0 1086.3 jit_solution(5104642623732953517)
XLA Ops:
  8.2 4.9 collective-permute-start.1
  13.2 1.9 collective-permute-start
  15.2 2.6 constant_dynamic-update-slice_fusion.1
  20.3 4.0 collective-permute-start.3
  25.3 12.3 %divide_add_fusion.1 = f32[64,128,128]{2,1,0:T(8,128)S(1)} fusion(f32[64,128,128]{2,1,0:T(8,128)S(1)} %copy-done.1, f32[66,128,128]{2,1,0:T(8,128)S(1)} %constant_dynamic-update-slice_fusion, f32[66,1,128]{2,1,0:T(1,128)S(1)} %collective-permute-done.3, f32[66,1,128]{2,1,0:T(1,128)S(1)} %collective-permute-done.2, ...), kind=kLoop, calls=%fused_computation.77 | loop fusion | flops 63963136 | bytes 17106944 | tf_op jit(solution)/shard_map/add | solution.py:40
  37.6 1.9 collective-permute-start.4
  39.5 3.9 collective-permute-start.5
  46.2 4.6 collective-permute-start.7
  51.7 14.4 %divide_add_fusion = f32[64,128,128]{2,1,0:T(8,128)S(1)} fusion(f32[64,128,128]{2,1,0:T(8,128)S(1)} %divide_add_fusion.1, f32[1,128,128]{2,1,0:T(8,128)S(1)} %collective-permute-done.4, f32[1,128,128]{2,1,0:T(8,128)S(1)} %collective-permute-done.5, f32[66,1,128]{2,1,0:T(1,128)S(1)} %collective-permute-done.7, f32[66,1,128]{2,1,0:T(1,128)S(1)} %collective-permute-done.6, ...), kind=kLoop, calls=%fused_computation.76 | loop fusion | flops 68157440 | bytes 12781568 | tf_op jit(solution)/shard_map/add | solution.py:40
  66.2 2.0 copy-done.3
  68.2 3.6 convolution_bitcast_fusion
  71.8 2.6 copy.106
  74.6 5.1 collective-permute-start.8
  79.7 2.1 collective-permute-start.9
  86.4 3.3 fusion.52
  89.8 904.3 %all-gather.2.cloned.1.call-done = f32[3,262144]{0,1:T(8,128)} async-done(((f32[3,8192]{0,1:T(8,128)}), f32[3,262144]{0,1:T(8,128)}) %all-gather.2.cloned.1.call-update) | async-done | bytes 3145744 | tf_op jit(solution)/shard_map/all_gather | solution.py:82
  994.1 59.9 %gather_fusion = f32[4096,3]{1,0:T(8,128)} fusion(f32[3,262144]{0,1:T(8,128)} %all-gather.2.cloned.1.call-done, s32[4096]{0:T(1024)S(1)} %broadcast_clamp_fusion), kind=kCustom, calls=%fused_computation | custom fusion | bytes 114688 | tf_op jit(solution)/shard_map/jit(_take)/gather | solution.py:83
  1054.0 2.2 copy.107
  1056.2 5.0 multiply_reduce_fusion.2
  1061.6 3.3 collective-permute-start.10
  1064.8 2.1 collective-permute-start.11
  1067.0 2.7 collective-permute-done.11
  1069.7 3.3 fusion.48
  1075.0 3.4 multiply_reduce_fusion
  (62 shorter events, 16.2 us)
Async XLA Ops:
  7.2 77.4 %copy-start = (f32[1,32,128,128]{3,2,1,0:T(8,128)S(1)}, f32[1,32,128,128]{3,2,1,0:T(8,128)}, u32[]{:S(2)}) copy-start(f32[1,32,128,128]{3,2,1,0:T(8,128)} %param.17) | copy-start | bytes 6291460
  7.2 986.9 %all-gather.2.cloned.1.call-start = ((), (), s32[]{:S(2)}) async-start(), calls=%async_computation | async-start | bytes 138412032 | tf_op jit(solution)/shard_map/all_gather | solution.py:82
  8.2 6.9 collective-permute-start.1
  13.2 5.6 collective-permute-start
  15.1 10.1 copy-start.1
  15.2 10.1 copy-start.2
  18.8 5.4 collective-permute-start.2
  20.3 5.0 collective-permute-start.3
  37.6 5.9 collective-permute-start.4
  39.5 5.3 collective-permute-start.5
  44.8 5.9 collective-permute-start.6
  46.1 22.0 %copy-start.7 = (f32[3,128]{1,0:T(4,128)S(1)}, f32[3,128]{1,0:T(4,128)}, u32[]{:S(2)}) copy-start(f32[3,128]{1,0:T(4,128)} %param.11) | copy-start | bytes 4612
  46.2 5.6 collective-permute-start.7
  66.1 2.0 copy-start.3
  71.8 2.7 copy-start.5
  71.8 10.1 copy-start.6
  71.8 10.1 copy-start.8
  71.8 10.1 copy-start.9
  74.6 8.2 collective-permute-start.8
  79.7 4.9 collective-permute-start.9
  1061.2 13.8 %copy-start.4 = (f32[1,32,128,128]{3,2,1,0:T(8,128)S(1)}, f32[1,32,128,128]{3,2,1,0:T(8,128)}, u32[]{:S(2)}) copy-start(f32[1,32,128,128]{3,2,1,0:T(8,128)} %param.16) | copy-start | bytes 6291460
  1061.6 5.4 collective-permute-start.10
  1064.8 4.9 collective-permute-start.11
Sparse Core Ops, SparseCore 0:
  74.6 919.3 all-gather.1
where the time goes:
time: 1090 us
  waiting for transfers between devices  913 us (84%)
  local copies, waits for them, and re-layouts  70.6 us (6%)
  starting transfers between devices  36.7 us (3%)
  other arithmetic  28.2 us (3%)
  matrix products  23.2 us (2%)
  between operations  14.5 us (1%)
    all_gather x1, waiting for transfers between devices, per_device(): table = lax.all_gather(surface, 'track', axis=1, tiled=True)  904 us
    gather x2, local copies, waits for them, and re-layouts, per_device(): applied = jnp.take(table, cells, axis=1)  62.1 us
    add x2, other arithmetic, relax_sweep(): return center + 0.8 * numer / denom  26.7 us
    ppermute x6, starting transfers between devices, extended(): lax.ppermute(lax.slice_in_dim(block, block.shape[dim] - width, None, axis...  25.8 us
  transfers between devices with their start and end apart: 13, of which 7 were waited for; matrix products, arithmetic and copies ran while one was open for 1% of the time, Pallas kernels for 0%

commit v1 on v0

--- a/solution.py
+++ b/solution.py
@@ -79,7 +79,10 @@
         3, rows_x * rows_y
     )
     cells = footprint[0]
-    table = lax.all_gather(surface, "track", axis=1, tiled=True)
+    devices = lax.axis_size("track")
+    blocks = jnp.stack([surface for _ in range(devices)])
+    blocks = lax.all_to_all(blocks, "track", split_axis=0, concat_axis=0)
+    table = jnp.concatenate(blocks, axis=1)
     applied = jnp.take(table, cells, axis=1)
     n_prof = temp_profile.shape[0]
     onehot = (temp_index[0][None, :] == jnp.arange(n_prof, dtype=jnp.int32)[:, None]).astype(

time: 1090 us -> 299 us (0.27)
  the two profiles are of different devices: /device:TPU:1 before, /device:TPU:5 now
where the time goes in v1:
time: 299 us; the launch traced here: 298 us
  local copies, waits for them, and re-layouts  130 us (43%)
  waiting for transfers between devices  61.3 us (21%)
  starting transfers between devices  54.4 us (18%)
  other arithmetic  28.3 us (9%)
  matrix products  23.2 us (8%)
    gather x2, local copies, waits for them, and re-layouts, per_device(): applied = jnp.take(table, cells, axis=1)  61.7 us
    reshape x1, local copies, waits for them, and re-layouts, per_device(): table = jnp.concatenate(blocks, axis=1)  59.3 us
    all_to_all x1, waiting for transfers between devices, per_device(): blocks = lax.all_to_all(blocks, 'track', split_axis=0, concat_axis=0)  29.9 us
    add x2, other arithmetic, relax_sweep(): return center + 0.8 * numer / denom  26.7 us
    ppermute x6, starting transfers between devices, extended(): lax.ppermute(lax.slice_in_dim(block, block.shape[dim] - width, None, axis...  24.9 us
    ppermute x6, waiting for transfers between devices, extended(): lax.ppermute(lax.slice_in_dim(block, 0, width, axis=dim), axis, backward)  19.1 us
    all_to_all x1, starting transfers between devices, per_device(): blocks = lax.all_to_all(blocks, 'track', split_axis=0, concat_axis=0)  16.5 us
    ppermute x6, starting transfers between devices, extended(): lax.ppermute(lax.slice_in_dim(block, 0, width, axis=dim), axis, backward)  13 us
  transfers between devices with their start and end apart: 13, of which 8 were waited for; matrix products, arithmetic and copies ran while one was open for 3% of the time, Pallas kernels for 0%

profile of v1, /device:TPU:5, one launch (start us, length us, event | category | flops | bytes accessed | tf_op | source)
XLA Modules:
  0.0 297.8 jit_solution(9152217867691268218)
XLA Ops:
  1.7 4.1 %collective-permute-start.1 = (f32[1,128,128]{2,1,0:T(8,128)S(1)}, f32[1,128,128]{2,1,0:T(8,128)S(1)}, u32[]{:S(2)}, u32[]{:S(2)}) collective-permute-start(f32[1,128,128]{2,1,0:T(8,128)S(1)} %get-tuple-element.21), channel_id=1, source_target_pairs={{0,32},{32,64},{64,96},{1,33},{33,65},{65,97},{2,34},{34,66},{66,9... | collective-permute-start | bytes 196616 | tf_op jit(solution)/shard_map/ppermute | solution.py:14
  7.8 2.6 constant_dynamic-update-slice_fusion.1
  11.4 2.3 collective-permute-start.2
  13.7 3.1 %collective-permute-start.3 = (f32[66,1,128]{2,1,0:T(1,128)S(1)}, f32[66,1,128]{2,1,0:T(1,128)S(1)}, u32[]{:S(2)}, u32[]{:S(2)}) collective-permute-start(f32[66,1,128]{2,1,0:T(1,128)S(1)} %get-tuple-element.17), channel_id=1, source_target_pairs={{0,1},{1,2},{2,3},{3,4},{4,5},{5,6},{6,7},{7,8},{8,9},{9,10},{10,1... | collective-permute-start | bytes 101384 | tf_op jit(solution)/shard_map/ppermute | solution.py:14
  18.4 12.3 %divide_add_fusion.1 = f32[64,128,128]{2,1,0:T(8,128)S(1)} fusion(f32[64,128,128]{2,1,0:T(8,128)S(1)} %copy-done.1, f32[66,128,128]{2,1,0:T(8,128)S(1)} %constant_dynamic-update-slice_fusion, f32[66,1,128]{2,1,0:T(1,128)S(1)} %collective-permute-done.3, f32[66,1,128]{2,1,0:T(1,128)S(1)} %collective-permute-done.2, ...), kind=kLoop, calls=%fused_computation.77 | loop fusion | flops 63963136 | bytes 17106944 | tf_op jit(solution)/shard_map/add | solution.py:40
  32.7 4.2 %collective-permute-start.5 = (f32[1,128,128]{2,1,0:T(8,128)S(1)}, f32[1,128,128]{2,1,0:T(8,128)S(1)}, u32[]{:S(2)}, u32[]{:S(2)}) collective-permute-start(f32[1,128,128]{2,1,0:T(8,128)S(1)} %get-tuple-element.18), channel_id=1, source_target_pairs={{0,32},{32,64},{64,96},{1,33},{33,65},{65,97},{2,34},{34,66},{66,9... | collective-permute-start | bytes 196616 | tf_op jit(solution)/shard_map/ppermute | solution.py:14
  40.4 5.4 %collective-permute-start.7 = (f32[66,1,128]{2,1,0:T(1,128)S(1)}, f32[66,1,128]{2,1,0:T(1,128)S(1)}, u32[]{:S(2)}, u32[]{:S(2)}) collective-permute-start(f32[66,1,128]{2,1,0:T(1,128)S(1)} %get-tuple-element.15), channel_id=1, source_target_pairs={{0,1},{1,2},{2,3},{3,4},{4,5},{5,6},{6,7},{7,8},{8,9},{9,10},{10,1... | collective-permute-start | bytes 101384 | tf_op jit(solution)/shard_map/ppermute | solution.py:14
  46.8 14.4 %divide_add_fusion = f32[64,128,128]{2,1,0:T(8,128)S(1)} fusion(f32[64,128,128]{2,1,0:T(8,128)S(1)} %divide_add_fusion.1, f32[1,128,128]{2,1,0:T(8,128)S(1)} %collective-permute-done.4, f32[1,128,128]{2,1,0:T(8,128)S(1)} %collective-permute-done.5, f32[66,1,128]{2,1,0:T(1,128)S(1)} %collective-permute-done.7, f32[66,1,128]{2,1,0:T(1,128)S(1)} %collective-permute-done.6, ...), kind=kLoop, calls=%fused_computation.76 | loop fusion | flops 68157440 | bytes 12781568 | tf_op jit(solution)/shard_map/add | solution.py:40
  63.3 3.6 %convolution_bitcast_fusion = f32[3,8192]{1,0:T(4,128)S(1)} fusion(f32[64,128,128]{2,1,0:T(8,128)S(1)} %divide_add_fusion, f32[3,128]{1,0:T(4,128)S(1)} %copy-done.7), kind=kOutput, calls=%fused_computation.5 | convolution fusion | flops 37748736 | bytes 4294144 | tf_op jit(solution)/shard_map/kz,xyz->kxy/dot_general | solution.py:78
  66.9 2.9 stack.55
  69.8 16.5 %all-to-all-start = ((f32[32,3,8192]{2,1,0:T(4,128)}), f32[32,3,8192]{2,1,0:T(4,128)}, u32[]{:S(2)}, u32[]{:S(2)}) async-start(f32[32,3,8192]{2,1,0:T(4,128)} %stack.55), calls=%async_computation | async-start | bytes 8388608 | tf_op jit(solution)/shard_map/all_to_all | solution.py:84
  86.4 6.0 %collective-permute-start.8 = (f32[3,128]{1,0:T(4,128)S(1)}, f32[3,128]{1,0:T(4,128)S(1)}, u32[]{:S(2)}, u32[]{:S(2)}) collective-permute-start(f32[3,128]{1,0:T(4,128)S(1)} %get-tuple-element.24), channel_id=1, source_target_pairs={{0,32},{32,64},{64,96},{1,33},{33,65},{65,97},{2,34},{34,66},{66,9... | collective-permute-start | bytes 4616 | tf_op jit(solution)/shard_map/ppermute | solution.py:14
  95.4 8.4 %collective-permute-done.8 = f32[3,128]{1,0:T(4,128)S(1)} collective-permute-done((f32[3,128]{1,0:T(4,128)S(1)}, f32[3,128]{1,0:T(4,128)S(1)}, u32[]{:S(2)}, u32[]{:S(2)}) %collective-permute-start.8) | collective-permute-done | bytes 1568 | tf_op jit(solution)/shard_map/ppermute | solution.py:14
  103.8 15.9 %collective-permute-done.9 = f32[3,128]{1,0:T(4,128)S(1)} collective-permute-done((f32[3,128]{1,0:T(4,128)S(1)}, f32[3,128]{1,0:T(4,128)S(1)}, u32[]{:S(2)}, u32[]{:S(2)}) %collective-permute-start.9) | collective-permute-done | bytes 1568 | tf_op jit(solution)/shard_map/ppermute | solution.py:17
  121.5 3.3 %fusion.52 = f32[32,3,128]{2,1,0:T(4,128)S(1)} fusion(f32[1,32,128,128]{3,2,1,0:T(8,128)S(1)} %copy-done, f32[3,128]{1,0:T(4,128)S(1)} %collective-permute-done.9, f32[3,4096]{1,0:T(4,128)S(1)} %bitcast.166, f32[3,128]{1,0:T(4,128)S(1)} %collective-permute-done.8), kind=kOutput, calls=%fused_computation.84 | convolution fusion | flops 18900480 | bytes 2198528 | tf_op jit(solution)/shard_map/kij,ckj->cki/dot_general | solution.py:101
  124.9 29.9 %all-to-all-done = f32[32,3,8192]{2,1,0:T(4,128)} async-done(((f32[32,3,8192]{2,1,0:T(4,128)}), f32[32,3,8192]{2,1,0:T(4,128)}, u32[]{:S(2)}, u32[]{:S(2)}) %all-to-all-start) | async-done | bytes 3145760 | tf_op jit(solution)/shard_map/all_to_all | solution.py:84
  154.8 59.3 %copy.106 = f32[3,32,8192]{0,2,1:T(8,128)} copy(f32[3,32,8192]{2,0,1:T(4,128)} %bitcast.5) | data formatting | bytes 6291456 | tf_op jit(solution)/shard_map/reshape | solution.py:85
  214.1 59.5 %gather_fusion = f32[4096,3]{1,0:T(8,128)} fusion(f32[3,262144]{0,1:T(8,128)} %bitcast.6, s32[4096]{0:T(1024)S(1)} %broadcast_clamp_fusion), kind=kCustom, calls=%fused_computation | custom fusion | bytes 114688 | tf_op jit(solution)/shard_map/jit(_take)/gather | solution.py:86
  273.6 2.2 copy.107
  275.8 5.0 %multiply_reduce_fusion.2 = (f32[4096]{0:T(1024)S(1)}, f32[3,4096]{1,0:T(4,128)S(1)}) fusion(f32[3,1,4096]{2,1,0:T(1,128)S(1)} %copy-done.5, f32[3,4096]{1,0:T(4,128)S(1)} %bitcast.167, f32[4096]{0:T(1024)S(1)} %subtract_multiply_fusion.1, f32[32,3,128]{2,1,0:T(4,128)S(1)} %fusion.50, f32[32,3,128]{2,1,0:T(4,128)S(1)} %fusion.52, ...), kind=kOutput, calls=%fused_computation.115 | convolution fusion | flops 18994688 | bytes 2432000 | tf_op jit(solution)/shard_map/kij,ckj->cki/dot_general | solution.py:100
  283.2 2.6 collective-permute-start.11
  285.9 2.2 collective-permute-done.11
  288.1 3.3 %fusion.48 = f32[32,3,128]{2,1,0:T(4,128)S(1)} fusion(f32[1,32,128,128]{3,2,1,0:T(8,128)S(1)} %copy-done, f32[3,128]{1,0:T(4,128)S(1)} %collective-permute-done.11, f32[3,4096]{1,0:T(4,128)S(1)} %get-tuple-element.8, f32[3,128]{1,0:T(4,128)S(1)} %collective-permute-done.10), kind=kOutput, calls=%fused_computation.80 | convolution fusion | flops 18900480 | bytes 2198528 | tf_op jit(solution)/shard_map/kij,ckj->cki/dot_general | solution.py:101
  293.3 3.4 %multiply_reduce_fusion = (f32[4096]{0:T(1024)S(1)}, f32[3,4096]{1,0:T(4,128)S(1)}) fusion(f32[3,4096]{1,0:T(4,128)S(1)} %get-tuple-element.8, f32[4096]{0:T(1024)S(1)} %subtract_multiply_fusion, f32[32,3,128]{2,1,0:T(4,128)S(1)} %fusion.46, f32[32,3,128]{2,1,0:T(4,128)S(1)} %fusion.48, f32[1,32,128,128]{3,2,1,0:T(8,128)S(1)} %copy-done.4, ...), kind=kOutput, calls=%fused_computation.113 | convolution fusion | flops 18994688 | bytes 2382848 | tf_op jit(solution)/shard_map/kij,ckj->cki/dot_general | solution.py:100
  (62 shorter events, 24.2 us)
Async XLA Ops:
  0.6 119.0 %copy-start = (f32[1,32,128,128]{3,2,1,0:T(8,128)S(1)}, f32[1,32,128,128]{3,2,1,0:T(8,128)}, u32[]{:S(2)}) copy-start(f32[1,32,128,128]{3,2,1,0:T(8,128)} %param.17) | copy-start | bytes 6291460
  1.7 6.0 %collective-permute-start.1 = (f32[1,128,128]{2,1,0:T(8,128)S(1)}, f32[1,128,128]{2,1,0:T(8,128)S(1)}, u32[]{:S(2)}, u32[]{:S(2)}) collective-permute-start(f32[1,128,128]{2,1,0:T(8,128)S(1)} %get-tuple-element.21), channel_id=1, source_target_pairs={{0,32},{32,64},{64,96},{1,33},{33,65},{65,97},{2,34},{34,66},{66,9... | collective-permute-start | bytes 196616 | tf_op jit(solution)/shard_map/ppermute | solution.py:14
  5.8 5.6 %collective-permute-start = (f32[1,128,128]{2,1,0:T(8,128)S(1)}, f32[1,128,128]{2,1,0:T(8,128)S(1)}, u32[]{:S(2)}, u32[]{:S(2)}) collective-permute-start(f32[1,128,128]{2,1,0:T(8,128)S(1)} %get-tuple-element.20), channel_id=1, source_target_pairs={{32,0},{64,32},{96,64},{33,1},{65,33},{97,65},{34,2},{66,34},{98,6... | collective-permute-start | bytes 196616 | tf_op jit(solution)/shard_map/ppermute | solution.py:17
  7.7 10.7 %copy-start.1 = (f32[64,128,128]{2,1,0:T(8,128)S(1)}, f32[64,128,128]{2,1,0:T(8,128)}, u32[]{:S(2)}) copy-start(f32[64,128,128]{2,1,0:T(8,128)} %param.9) | copy-start | bytes 12582916
  7.8 10.7 %copy-start.2 = (f32[64,128,128]{2,1,0:T(8,128)S(1)}, f32[64,128,128]{2,1,0:T(8,128)}, u32[]{:S(2)}) copy-start(f32[64,128,128]{2,1,0:T(8,128)} %param.10) | copy-start | bytes 12582916
  11.4 5.4 %collective-permute-start.2 = (f32[66,1,128]{2,1,0:T(1,128)S(1)}, f32[66,1,128]{2,1,0:T(1,128)S(1)}, u32[]{:S(2)}, u32[]{:S(2)}) collective-permute-start(f32[66,1,128]{2,1,0:T(1,128)S(1)} %get-tuple-element.16), channel_id=1, source_target_pairs={{1,0},{2,1},{3,2},{4,3},{5,4},{6,5},{7,6},{8,7},{9,8},{10,9},{11,1... | collective-permute-start | bytes 101384 | tf_op jit(solution)/shard_map/ppermute | solution.py:17
  13.7 4.7 %collective-permute-start.3 = (f32[66,1,128]{2,1,0:T(1,128)S(1)}, f32[66,1,128]{2,1,0:T(1,128)S(1)}, u32[]{:S(2)}, u32[]{:S(2)}) collective-permute-start(f32[66,1,128]{2,1,0:T(1,128)S(1)} %get-tuple-element.17), channel_id=1, source_target_pairs={{0,1},{1,2},{2,3},{3,4},{4,5},{5,6},{6,7},{7,8},{8,9},{9,10},{10,1... | collective-permute-start | bytes 101384 | tf_op jit(solution)/shard_map/ppermute | solution.py:14
  30.7 6.2 %collective-permute-start.4 = (f32[1,128,128]{2,1,0:T(8,128)S(1)}, f32[1,128,128]{2,1,0:T(8,128)S(1)}, u32[]{:S(2)}, u32[]{:S(2)}) collective-permute-start(f32[1,128,128]{2,1,0:T(8,128)S(1)} %get-tuple-element.19), channel_id=1, source_target_pairs={{32,0},{64,32},{96,64},{33,1},{65,33},{97,65},{34,2},{66,34},{98,6... | collective-permute-start | bytes 196616 | tf_op jit(solution)/shard_map/ppermute | solution.py:17
  32.7 5.6 %collective-permute-start.5 = (f32[1,128,128]{2,1,0:T(8,128)S(1)}, f32[1,128,128]{2,1,0:T(8,128)S(1)}, u32[]{:S(2)}, u32[]{:S(2)}) collective-permute-start(f32[1,128,128]{2,1,0:T(8,128)S(1)} %get-tuple-element.18), channel_id=1, source_target_pairs={{0,32},{32,64},{64,96},{1,33},{33,65},{65,97},{2,34},{34,66},{66,9... | collective-permute-start | bytes 196616 | tf_op jit(solution)/shard_map/ppermute | solution.py:14
  38.3 7.6 %collective-permute-start.6 = (f32[66,1,128]{2,1,0:T(1,128)S(1)}, f32[66,1,128]{2,1,0:T(1,128)S(1)}, u32[]{:S(2)}, u32[]{:S(2)}) collective-permute-start(f32[66,1,128]{2,1,0:T(1,128)S(1)} %get-tuple-element.14), channel_id=1, source_target_pairs={{1,0},{2,1},{3,2},{4,3},{5,4},{6,5},{7,6},{8,7},{9,8},{10,9},{11,1... | collective-permute-start | bytes 101384 | tf_op jit(solution)/shard_map/ppermute | solution.py:17
  40.4 22.8 %copy-start.7 = (f32[3,128]{1,0:T(4,128)S(1)}, f32[3,128]{1,0:T(4,128)}, u32[]{:S(2)}) copy-start(f32[3,128]{1,0:T(4,128)} %param.11) | copy-start | bytes 4612
  40.4 6.4 %collective-permute-start.7 = (f32[66,1,128]{2,1,0:T(1,128)S(1)}, f32[66,1,128]{2,1,0:T(1,128)S(1)}, u32[]{:S(2)}, u32[]{:S(2)}) collective-permute-start(f32[66,1,128]{2,1,0:T(1,128)S(1)} %get-tuple-element.15), channel_id=1, source_target_pairs={{0,1},{1,2},{2,3},{3,4},{4,5},{5,6},{6,7},{7,8},{8,9},{9,10},{10,1... | collective-permute-start | bytes 101384 | tf_op jit(solution)/shard_map/ppermute | solution.py:14
  61.2 2.0 copy-start.3
  69.8 16.5 %copy-start.5 = (f32[3,1,4096]{2,1,0:T(1,128)S(1)}, f32[3,1,4096]{2,1,0:T(1,128)}, u32[]{:S(2)}) copy-start(f32[3,1,4096]{2,1,0:T(1,128)} %param.12) | copy-start | bytes 147460
  69.8 24.7 %copy-start.6 = (s32[1,4096]{1,0:T(1,128)S(1)}, s32[1,4096]{1,0:T(1,128)}, u32[]{:S(2)}) copy-start(s32[1,4096]{1,0:T(1,128)} %param.13) | copy-start | bytes 49156
  69.8 24.8 %copy-start.8 = (s32[1,4096]{1,0:T(1,128)S(1)}, s32[1,4096]{1,0:T(1,128)}, u32[]{:S(2)}) copy-start(s32[1,4096]{1,0:T(1,128)} %param.14) | copy-start | bytes 49156
  69.8 24.8 %copy-start.9 = (f32[128]{0:T(128)S(1)}, f32[128]{0:T(128)}, u32[]{:S(2)}) copy-start(f32[128]{0:T(128)} %param.15) | copy-start | bytes 1540
  69.8 85.0 %all-to-all-start = ((f32[32,3,8192]{2,1,0:T(4,128)}), f32[32,3,8192]{2,1,0:T(4,128)}, u32[]{:S(2)}, u32[]{:S(2)}) async-start(f32[32,3,8192]{2,1,0:T(4,128)} %stack.55), calls=%async_computation | async-start | bytes 8388608 | tf_op jit(solution)/shard_map/all_to_all | solution.py:84
  86.4 17.4 %collective-permute-start.8 = (f32[3,128]{1,0:T(4,128)S(1)}, f32[3,128]{1,0:T(4,128)S(1)}, u32[]{:S(2)}, u32[]{:S(2)}) collective-permute-start(f32[3,128]{1,0:T(4,128)S(1)} %get-tuple-element.24), channel_id=1, source_target_pairs={{0,32},{32,64},{64,96},{1,33},{33,65},{65,97},{2,34},{34,66},{66,9... | collective-permute-start | bytes 4616 | tf_op jit(solution)/shard_map/ppermute | solution.py:14
  92.3 27.3 %collective-permute-start.9 = (f32[3,128]{1,0:T(4,128)S(1)}, f32[3,128]{1,0:T(4,128)S(1)}, u32[]{:S(2)}, u32[]{:S(2)}) collective-permute-start(f32[3,128]{1,0:T(4,128)S(1)} %get-tuple-element.25), channel_id=1, source_target_pairs={{32,0},{64,32},{96,64},{33,1},{65,33},{97,65},{34,2},{66,34},{98,6... | collective-permute-start | bytes 4616 | tf_op jit(solution)/shard_map/ppermute | solution.py:17
  280.8 12.6 %copy-start.4 = (f32[1,32,128,128]{3,2,1,0:T(8,128)S(1)}, f32[1,32,128,128]{3,2,1,0:T(8,128)}, u32[]{:S(2)}) copy-start(f32[1,32,128,128]{3,2,1,0:T(8,128)} %param.16) | copy-start | bytes 6291460
  281.2 4.7 %collective-permute-start.10 = (f32[3,128]{1,0:T(4,128)S(1)}, f32[3,128]{1,0:T(4,128)S(1)}, u32[]{:S(2)}, u32[]{:S(2)}) collective-permute-start(f32[3,128]{1,0:T(4,128)S(1)} %get-tuple-element.22), channel_id=1, source_target_pairs={{0,32},{32,64},{64,96},{1,33},{33,65},{65,97},{2,34},{34,66},{66,9... | collective-permute-start | bytes 4616 | tf_op jit(solution)/shard_map/ppermute | solution.py:14
  283.2 4.9 %collective-permute-start.11 = (f32[3,128]{1,0:T(4,128)S(1)}, f32[3,128]{1,0:T(4,128)S(1)}, u32[]{:S(2)}, u32[]{:S(2)}) collective-permute-start(f32[3,128]{1,0:T(4,128)S(1)} %get-tuple-element.23), channel_id=1, source_target_pairs={{32,0},{64,32},{96,64},{33,1},{65,33},{97,65},{34,2},{66,34},{98,6... | collective-permute-start | bytes 4616 | tf_op jit(solution)/shard_map/ppermute | solution.py:17
